TPU v7x, 256 devices: a whole 4x4x8 slice. The times are simulated.
256 devices in a mesh: gx: 16 (over y_lo, z), gy: 16 (over x, y_hi, core).
Axes of the slice: x: 4, y: 4 (y_hi: 2, y_lo: 2; y = y_hi * 2 + y_lo), z: 8, core: 2. Of those that a mesh axis runs over, the one named last changes fastest.
Arguments:
- tokens: bfloat16 [4, 128, 128, 256], P(None, 'gx', 'gy'), may hold values from -6 to 6
- syndrome: int32 [4, 128, 128], P(None, 'gx', 'gy'), may hold values 0 or 1
- check_plan_step: int32 [4, 128, 128], P(None, 'gx', 'gy'), may hold values from 0 to 7
- offsets: int32 [6, 2], replicated, may hold values from 0 to 8, as said below
- flip_vector: float32 [256], replicated, may hold values from -3 to 3
- plan_step_embedding: float32 [8, 256], replicated, may hold values from -3 to 3
- gain_tanner: float32 [256], replicated, may hold values from 0.5 to 1.5
- w_query: bfloat16 [256, 256], replicated, may hold values from -0.375 to 0.375
- w_key_value: bfloat16 [256, 512], replicated, may hold values from -0.375 to 0.375
- w_merge: bfloat16 [256, 256], replicated, may hold values from -0.375 to 0.375
- gain_time: float32 [256], replicated, may hold values from 0.5 to 1.5
- w_temporal: bfloat16 [256, 768], replicated, may hold values from -0.375 to 0.375
- w_temporal_out: bfloat16 [256, 256], replicated, may hold values from -0.375 to 0.375
- gain_ffn: float32 [256], replicated, may hold values from 0.5 to 1.5
- w_ffn_up: bfloat16 [256, 1024], replicated, may hold values from -0.375 to 0.375
- w_ffn_down: bfloat16 [1024, 256], replicated, may hold values from -0.1875 to 0.1875
- cotangent: bfloat16 [4, 128, 128, 256], P(None, 'gx', 'gy'), may hold values from -6 to 6
Outputs:
- token_grad: bfloat16 [4, 128, 128, 256], P(None, 'gx', 'gy')
- grad_flip: float32 [256], replicated
- plan_step_gradient: float32 [8, 256], replicated
- grad_gain_tanner: float32 [256], replicated
- grad_query: float32 [256, 256], replicated
- grad_key_value: float32 [256, 512], replicated
- grad_merge: float32 [256, 256], replicated
- grad_gain_time: float32 [256], replicated
- grad_temporal: float32 [256, 768], replicated
- grad_temporal_out: float32 [256, 256], replicated
- grad_gain_ffn: float32 [256], replicated
- grad_up: float32 [256, 1024], replicated
- grad_down: float32 [1024, 256], replicated
Inputs may be any that keep to these rules, and one draw needn't show every extreme that they name: `offsets`: rows 0, 4 and 5 are (e, 0) and rows 1, 2 and 3 are (0, e), with e from 1 to 8; rows 0 and 3 have e = 8.
All inputs are finite; a program needn't handle non-finite values. No bound on the sum of `syndrome` on one device may be relied on, other than what follows from the above.
Results may differ from a plain program's by a relative error of at most 0.022.
Values may be sent and summed in bfloat16 or wider, within the bound.
A program may use at most 64 MiB of HBM per device.

v0:
```python
import math
import jax
import jax.numpy as jnp
from jax import lax
from jax.sharding import PartitionSpec as P

MODEL_WIDTH = 256
HEADDIM = 32
PLAN_STEP_COUNT = 8
MONOS = 6
MAXEXP = 8
EPS = 1e-05
CAP = 4.0
EXACT_PRECISION = lax.Precision.HIGHEST
ALONG_ROWS = (0, 4, 5)


def shifted(x, axis, by):
    count = lax.axis_size(axis)
    return lax.ppermute(x, axis, [(i, (i + by) % count) for i in range(count)])


def rms_norm(stream, gain):
    return stream * lax.rsqrt(jnp.mean(stream * stream, axis=-1, keepdims=True) + EPS) * gain


def matmul(inputs, weight):
    return lax.dot_general(
        inputs, weight, (((inputs.ndim - 1,), (0,)), ((), ())), preferred_element_type=jnp.float32
    )


def back_matmul(inputs, weight, grad_result):
    grad_low = grad_result.astype(jnp.bfloat16)
    grad_inputs = lax.dot_general(
        grad_low,
        weight,
        (((grad_low.ndim - 1,), (1,)), ((), ())),
        preferred_element_type=jnp.float32,
    )
    flat_inputs = inputs.reshape(-1, inputs.shape[-1])
    flat_grad = grad_low.reshape(-1, grad_low.shape[-1])
    grad_weight = lax.dot_general(
        flat_inputs, flat_grad, (((0,), (0,)), ((), ())), preferred_element_type=jnp.float32
    )
    return (grad_inputs, grad_weight)


def head_total(product):
    width = product.shape[-1]
    row_head = lax.broadcasted_iota(jnp.int32, (width, width), 0) // HEADDIM
    col_head = lax.broadcasted_iota(jnp.int32, (width, width), 1) // HEADDIM
    block = (row_head == col_head).astype(jnp.float32)
    return lax.dot_general(
        product, block, (((product.ndim - 1,), (0,)), ((), ())), precision=EXACT_PRECISION
    )


def attend(query, moved):
    weights = []
    for neighbour in moved:
        score = head_total(query * neighbour[..., :MODEL_WIDTH]) / math.sqrt(HEADDIM)
        weights.append(jnp.exp(CAP * jnp.tanh(score / CAP)))
    normalizer = weights[0]
    for weight in weights[1:]:
        normalizer = normalizer + weight
    mixed = jnp.zeros(query.shape, jnp.float32)
    for weight, neighbour in zip(weights, moved):
        mixed = mixed + weight / normalizer * neighbour[..., MODEL_WIDTH:]
    return mixed


def tanner_local(query, key_value, next_rows, next_cols, offsets):
    extended_rows = jnp.concatenate([key_value, next_rows], axis=1)
    extended_cols = jnp.concatenate([key_value, next_cols], axis=2)
    moved = [key_value]
    for index in range(MONOS):
        if index in ALONG_ROWS:
            moved.append(
                lax.dynamic_slice_in_dim(extended_rows, offsets[index, 0], key_value.shape[1], 1)
            )
        else:
            moved.append(
                lax.dynamic_slice_in_dim(extended_cols, offsets[index, 1], key_value.shape[2], 2)
            )
    return attend(query, moved)


def time_attend(packed):
    queries = packed[..., :MODEL_WIDTH]
    keys = packed[..., MODEL_WIDTH : 2 * MODEL_WIDTH]
    values = packed[..., 2 * MODEL_WIDTH :]
    outputs = []
    for later in range(packed.shape[0]):
        weights = []
        for earlier in range(later + 1):
            score = head_total(queries[later] * keys[earlier]) / math.sqrt(HEADDIM)
            weights.append(jnp.exp(CAP * jnp.tanh(score / CAP)))
        normalizer = weights[0]
        for weight in weights[1:]:
            normalizer = normalizer + weight
        mixed = jnp.zeros(queries.shape[1:], jnp.float32)
        for earlier in range(later + 1):
            mixed = mixed + weights[earlier] / normalizer * values[earlier]
        outputs.append(mixed)
    return jnp.stack(outputs, axis=0)


def on_device(
    tokens,
    syndrome,
    check_plan_step,
    offsets,
    flip_vector,
    plan_step_embedding,
    gain_tanner,
    w_query,
    w_key_value,
    w_merge,
    gain_time,
    w_temporal,
    w_temporal_out,
    gain_ffn,
    w_ffn_up,
    w_ffn_down,
    cotangent,
):
    plan_step_onehot = (
        check_plan_step[..., None] == jnp.arange(PLAN_STEP_COUNT, dtype=jnp.int32)
    ).astype(jnp.float32)
    syndrome_float = syndrome.astype(jnp.float32)
    embedded = (
        tokens.astype(jnp.float32)
        + syndrome_float[..., None] * flip_vector
        + jnp.dot(plan_step_onehot, plan_step_embedding, precision=EXACT_PRECISION)
    )
    normed_one, norm_one_back = jax.vjp(rms_norm, embedded, gain_tanner)
    hidden_one = normed_one.astype(jnp.bfloat16)
    query = matmul(hidden_one, w_query).astype(jnp.bfloat16)
    key_value = matmul(hidden_one, w_key_value).astype(jnp.bfloat16)
    next_rows = shifted(key_value, "gx", -1)
    next_cols = shifted(key_value, "gy", -1)

    def tanner_part(query_in, key_in, rows_in, cols_in):
        return tanner_local(query_in, key_in, rows_in, cols_in, offsets)

    mixed_float, tanner_back = jax.vjp(
        tanner_part,
        query.astype(jnp.float32),
        key_value.astype(jnp.float32),
        next_rows.astype(jnp.float32),
        next_cols.astype(jnp.float32),
    )
    mixed_one = mixed_float.astype(jnp.bfloat16)
    after_tanner = embedded + matmul(mixed_one, w_merge)
    normed_two, norm_two_back = jax.vjp(rms_norm, after_tanner, gain_time)
    hidden_two = normed_two.astype(jnp.bfloat16)
    packed = matmul(hidden_two, w_temporal).astype(jnp.bfloat16)
    mixed_time, time_back = jax.vjp(time_attend, packed.astype(jnp.float32))
    mixed_two = mixed_time.astype(jnp.bfloat16)
    after_time = after_tanner + matmul(mixed_two, w_temporal_out)
    normed_three, norm_three_back = jax.vjp(rms_norm, after_time, gain_ffn)
    hidden_three = normed_three.astype(jnp.bfloat16)
    before_act = matmul(hidden_three, w_ffn_up)
    activated_float, gelu_back = jax.vjp(jax.nn.gelu, before_act)
    activated = activated_float.astype(jnp.bfloat16)
    grad_output = cotangent.astype(jnp.float32)
    grad_act, grad_down = back_matmul(activated, w_ffn_down, grad_output)
    grad_before = gelu_back(grad_act)[0]
    grad_three, grad_up = back_matmul(hidden_three, w_ffn_up, grad_before)
    grad_norm_three, grad_gain_ffn = norm_three_back(grad_three)
    grad_after_time = grad_output + grad_norm_three
    grad_mixed_two, grad_temporal_out = back_matmul(mixed_two, w_temporal_out, grad_after_time)
    grad_packed = time_back(grad_mixed_two)[0]
    grad_two, grad_temporal = back_matmul(hidden_two, w_temporal, grad_packed)
    grad_norm_two, grad_gain_time = norm_two_back(grad_two)
    grad_after_tanner = grad_after_time + grad_norm_two
    scale = 1.0 / math.sqrt(
        tokens.shape[0]
        * tokens.shape[1]
        * tokens.shape[2]
        * lax.axis_size("gx")
        * lax.axis_size("gy")
    )
    grad_mixed_one, grad_merge = back_matmul(mixed_one, w_merge, grad_after_tanner)
    grad_query_out, grad_key_local, grad_rows, grad_cols = tanner_back(grad_mixed_one)
    back_rows = shifted(grad_rows.astype(jnp.bfloat16), "gx", 1).astype(grad_rows.dtype)
    back_cols = shifted(grad_cols.astype(jnp.bfloat16), "gy", 1).astype(grad_cols.dtype)
    grad_key_out = grad_key_local.at[:, :MAXEXP].add(back_rows)
    grad_key_out = grad_key_out.at[:, :, :MAXEXP].add(back_cols)
    grad_one_key, grad_key_value = back_matmul(hidden_one, w_key_value, grad_key_out)
    grad_one_query, grad_query = back_matmul(hidden_one, w_query, grad_query_out)
    grad_norm_one, grad_gain_tanner = norm_one_back(grad_one_query + grad_one_key)
    embedding_gradient = grad_after_tanner + grad_norm_one
    token_grad = embedding_gradient.astype(jnp.bfloat16)
    grad_flip = jnp.sum(syndrome_float[..., None] * embedding_gradient, axis=(0, 1, 2))
    plan_step_gradient = lax.dot_general(
        plan_step_onehot.reshape(-1, PLAN_STEP_COUNT),
        embedding_gradient.reshape(-1, MODEL_WIDTH),
        (((0,), (0,)), ((), ())),
        precision=EXACT_PRECISION,
    )
    summed = lax.psum(
        (
            grad_flip * scale,
            plan_step_gradient * scale,
            grad_gain_tanner * scale,
            grad_query * scale,
            grad_key_value * scale,
            grad_merge * scale,
            grad_gain_time * scale,
            grad_temporal * scale,
            grad_temporal_out * scale,
            grad_gain_ffn * scale,
            grad_up * scale,
            grad_down * scale,
        ),
        ("gx", "gy"),
    )
    return (
        token_grad,
        summed[0],
        summed[1],
        summed[2],
        summed[3],
        summed[4],
        summed[5],
        summed[6],
        summed[7],
        summed[8],
        summed[9],
        summed[10],
        summed[11],
    )


def solution(mesh):
    return jax.shard_map(
        on_device,
        mesh=mesh,
        in_specs=(
            P(None, "gx", "gy", None),
            P(None, "gx", "gy"),
            P(None, "gx", "gy"),
            P(),
            P(),
            P(),
            P(),
            P(),
            P(),
            P(),
            P(),
            P(),
            P(),
            P(),
            P(),
            P(),
            P(None, "gx", "gy", None),
        ),
        out_specs=(
            P(None, "gx", "gy", None),
            P(),
            P(),
            P(),
            P(),
            P(),
            P(),
            P(),
            P(),
            P(),
            P(),
            P(),
            P(),
        ),
        check_vma=False,
    )
```

profile of v0, /device:TPU:2, one launch (start us, length us, event | category | flops | bytes accessed | tf_op | source)
XLA Modules:
  0.0 368.0 jit_solution(12279995785802206643)
XLA Ops:
  8.7 1.3 multiply_reduce_fusion.9
  11.2 6.9 %collective-permute-start = (bf16[4,8,8,512]{3,2,1,0:T(8,128)(2,1)S(1)}, bf16[4,8,8,512]{3,2,1,0:T(8,128)(2,1)S(1)}, u32[]{:S(2)}, u32[]{:S(2)}) collective-permute-start(bf16[4,8,8,512]{3,2,1,0:T(8,128)(2,1)S(1)} %get-tuple-element.163), channel_id=1, source_target_pairs={{0,240},{16,0},{32,16},{48,32},{64,48},{80,64},{96,80},{112,96},{1... | collective-permute-start | bytes 786440 | tf_op jit(solution)/shard_map/ppermute | solution.py:20
  18.1 2.0 collective-permute-start.1
  47.4 0.9 fusion.12
  52.9 1.3 fusion.2
  54.2 1.1 multiply_reduce_fusion.1
  55.4 1.9 fusion.472
  60.5 1.4 fusion.1
  61.8 1.5 fusion
  63.4 1.6 fusion.485
  65.1 0.9 dynamic_update_slice.22
  66.1 1.2 add_add_fusion.1
  67.2 1.0 add_any.332
  68.3 1.2 add_add_fusion
  69.4 0.9 add_any.335
  75.4 0.9 fusion.13
  76.3 2.4 collective-permute-done.3
  78.7 6.3 %collective-permute-done.2 = bf16[4,8,8,512]{3,2,1,0:T(8,128)(2,1)S(1)} collective-permute-done((bf16[4,8,8,512]{3,2,1,0:T(8,128)(2,1)S(1)}, bf16[4,8,8,512]{3,2,1,0:T(8,128)(2,1)S(1)}, u32[]{:S(2)}, u32[]{:S(2)}) %collective-permute-start.2) | collective-permute-done | bytes 262176 | tf_op jit(solution)/shard_map/ppermute | solution.py:20
  85.2 1.1 fusion.4
  91.3 75.0 %all-reduce.47 = (f32[256]{0:T(256)}, f32[8,256]{1,0:T(8,128)}, f32[256]{0:T(256)}, f32[256]{0:T(256)}, f32[256]{0:T(256)}) all-reduce(f32[256]{0:T(256)S(1)} %broadcast_multiply_fusion.3, f32[8,256]{1,0:T(8,128)S(1)} %fusion.26, f32[256]{0:T(256)S(1)} %broadcast_multiply_fusion.2, ...), channel_id=1, replica_groups=mesh['gx'=16,'gy'=16] {'gx','gy'}, use_global_device_ids=true, to_apply=%region_7.8 | all-reduce | flops 3072 | bytes 24576 | tf_op jit(solution)/shard_map/psum | solution.py:203
  166.3 187.0 %all-reduce.51.cloned.1.call-done = (f32[256,256]{1,0:T(8,128)}, f32[256,512]{1,0:T(8,128)}, f32[256,256]{1,0:T(8,128)}, f32[256,768]{1,0:T(8,128)}, f32[256,256...) async-done(((f32[256,256]{1,0:T(8,128)}, f32[256,512]{1,0:T(8,128)}, f32[256,256]{1,0:T(8,128)}, f32[256,768]{1,0:T(8,128)}, f32[256,256]{1,0:T(8,128)}, ...) | async-done | bytes 4194320 | tf_op jit(solution)/shard_map/psum | solution.py:203
  353.2 1.7 copy.62
  358.6 1.0 copy.67
  360.2 1.0 copy.68
  (176 shorter events, 40.1 us)
Async XLA Ops:
  7.2 36.4 %copy-start = (bf16[256,1024]{1,0:T(8,128)(2,1)S(1)}, bf16[256,1024]{1,0:T(8,128)(2,1)}, u32[]{:S(2)}) copy-start(bf16[256,1024]{1,0:T(8,128)(2,1)} %param.39) | copy-start | bytes 1572868
  7.2 1.4 copy-start.29
  7.2 1.4 copy-start.38
  7.2 1.4 copy-start.35
  7.2 346.0 %all-reduce.51.cloned.1.call-start = ((), (), s32[]{:S(2)}) async-start(), calls=%async_computation | async-start | bytes 8388608 | tf_op jit(solution)/shard_map/psum | solution.py:203
  8.6 1.9 copy-start.33
  10.9 21.5 %copy-start.10 = (bf16[256,256]{1,0:T(8,128)(2,1)S(1)}, bf16[256,256]{1,0:T(8,128)(2,1)}, u32[]{:S(2)}) copy-start(bf16[256,256]{1,0:T(8,128)(2,1)} %param.32) | copy-start | bytes 393220
  11.2 9.0 %copy-start.32 = (s32[6,2]{0,1:T(2,128)S(1)}, s32[6,2]{0,1:T(2,128)}, u32[]{:S(2)}) copy-start(s32[6,2]{0,1:T(2,128)} %param.28) | copy-start | bytes 148
  11.2 21.5 %collective-permute-start = (bf16[4,8,8,512]{3,2,1,0:T(8,128)(2,1)S(1)}, bf16[4,8,8,512]{3,2,1,0:T(8,128)(2,1)S(1)}, u32[]{:S(2)}, u32[]{:S(2)}) collective-permute-start(bf16[4,8,8,512]{3,2,1,0:T(8,128)(2,1)S(1)} %get-tuple-element.163), channel_id=1, source_target_pairs={{0,240},{16,0},{32,16},{48,32},{64,48},{80,64},{96,80},{112,96},{1... | collective-permute-start | bytes 786440 | tf_op jit(solution)/shard_map/ppermute | solution.py:20
  18.1 14.6 %collective-permute-start.1 = (bf16[4,8,8,512]{3,2,1,0:T(8,128)(2,1)S(1)}, bf16[4,8,8,512]{3,2,1,0:T(8,128)(2,1)S(1)}, u32[]{:S(2)}, u32[]{:S(2)}) collective-permute-start(bf16[4,8,8,512]{3,2,1,0:T(8,128)(2,1)S(1)} %get-tuple-element.163), channel_id=1, source_target_pairs={{0,15},{1,0},{2,1},{3,2},{4,3},{5,4},{6,5},{7,6},{8,7},{9,8},{10,9... | collective-permute-start | bytes 786440 | tf_op jit(solution)/shard_map/ppermute | solution.py:20
  20.8 39.2 %copy-start.19 = (pred[256]{0:T(512)(128)(4,1)}, pred[256]{0:T(512)(128)(4,1)S(1)}, u32[]{:S(2)}) copy-start(pred[256]{0:T(512)(128)(4,1)S(1)} %compare_and_fusion) | copy-start | bytes 772
  44.3 1.1 copy-start.40
  61.8 1.5 copy-start.20
  70.4 8.3 %collective-permute-start.3 = (bf16[4,8,8,512]{3,2,1,0:T(8,128)(2,1)S(1)}, bf16[4,8,8,512]{3,2,1,0:T(8,128)(2,1)S(1)}, u32[]{:S(2)}, u32[]{:S(2)}) collective-permute-start(bf16[4,8,8,512]{3,2,1,0:T(8,128)(2,1)S(1)} %split.34), channel_id=1, source_target_pairs={{0,1},{1,2},{2,3},{3,4},{4,5},{5,6},{6,7},{7,8},{8,9},{9,10},{10,1... | collective-permute-start | bytes 786440 | tf_op jit(solution)/shard_map/ppermute | solution.py:20
  70.5 1.0 copy-start.18
  73.6 11.4 %collective-permute-start.2 = (bf16[4,8,8,512]{3,2,1,0:T(8,128)(2,1)S(1)}, bf16[4,8,8,512]{3,2,1,0:T(8,128)(2,1)S(1)}, u32[]{:S(2)}, u32[]{:S(2)}) collective-permute-start(bf16[4,8,8,512]{3,2,1,0:T(8,128)(2,1)S(1)} %split.35), channel_id=1, source_target_pairs={{0,16},{16,32},{32,48},{48,64},{64,80},{80,96},{96,112},{112,128},... | collective-permute-start | bytes 786440 | tf_op jit(solution)/shard_map/ppermute | solution.py:20
  75.4 9.6 %copy-start.13 = (f32[4,8,8,256]{3,2,1,0:T(8,128)S(1)}, f32[4,8,8,256]{3,2,1,0:T(8,128)}, u32[]{:S(2)}) copy-start(f32[4,8,8,256]{3,2,1,0:T(8,128)} %get-tuple-element.105) | copy-start | bytes 786436
  86.2 1.4 copy-start.11
  353.2 1.7 copy-start.8
  355.0 1.1 copy-start.15
  355.0 1.8 copy-start.6
  356.8 1.1 copy-start.14
  356.8 1.8 copy-start.2
  358.6 1.6 copy-start.1
  (22 other events, 18.1 us)
Sparse Core Ops, SparseCore 0:
  86.4 266.8 all-reduce.50
where the time goes:
time: 369 us; the launch traced here: 368 us
  waiting for transfers between devices  196 us (53%)
  blocking collectives  75 us (20%)
  matrix products  32.2 us (9%)
  between operations  26.5 us (7%)
  local copies, waits for them, and re-layouts  23 us (6%)
  starting transfers between devices  9.18 us (2%)
  other arithmetic  6.54 us (2%)
    psum x1, waiting for transfers between devices, on_device(): lax.psum((grad_flip * scale, plan_step_gradient * scale, grad_gain_tanner...  187 us
    psum x1, blocking collectives, on_device(): lax.psum((grad_flip * scale, plan_step_gradient * scale, grad_gain_tanner...  75 us
    unnamed x89, local copies, waits for them, and re-layouts  19.3 us
    dot_general x34, matrix products, head_total(): lax.dot_general(product, block, (((product.ndim - 1,), (0,)), ((), ())),...  15.4 us
    ppermute x4, starting transfers between devices, shifted(): return lax.ppermute(x, axis, [(i, (i + by) % count) for i in range(count)])  9.15 us
    ppermute x4, waiting for transfers between devices, shifted(): return lax.ppermute(x, axis, [(i, (i + by) % count) for i in range(count)])  8.64 us
    dot_general x7, matrix products, back_matmul(): lax.dot_general(flat_inputs, flat_grad, (((0,), (0,)), ((), ())), preferr...  8.03 us
  transfers between devices with their start and end apart: 5, of which 3 were waited for; matrix products, arithmetic and copies ran while one was open for 1% of the time, Pallas kernels for 0%

commit v1 on v0

--- a/solution.py
+++ b/solution.py
@@ -201,21 +201,24 @@
         precision=EXACT_PRECISION,
     )
     summed = lax.psum(
-        (
-            grad_flip * scale,
-            plan_step_gradient * scale,
-            grad_gain_tanner * scale,
-            grad_query * scale,
-            grad_key_value * scale,
-            grad_merge * scale,
-            grad_gain_time * scale,
-            grad_temporal * scale,
-            grad_temporal_out * scale,
-            grad_gain_ffn * scale,
-            grad_up * scale,
-            grad_down * scale,
+        lax.psum(
+            (
+                grad_flip * scale,
+                plan_step_gradient * scale,
+                grad_gain_tanner * scale,
+                grad_query * scale,
+                grad_key_value * scale,
+                grad_merge * scale,
+                grad_gain_time * scale,
+                grad_temporal * scale,
+                grad_temporal_out * scale,
+                grad_gain_ffn * scale,
+                grad_up * scale,
+                grad_down * scale,
+            ),
+            "gx",
         ),
-        ("gx", "gy"),
+        "gy",
     )
     return (
         token_grad,

time: 369 us -> 409 us (1.11); the launches traced: 368 us -> 403 us
  blocking collectives: 75 us -> 119 us
  waiting for transfers between devices: 196 us -> 186 us
    psum x0 -> x1, blocking collectives: none -> 56.6 us  [on_device(): lax.psum(lax.psum((grad_flip * scale, plan_step_gradient * scale, grad_ga...]
    psum x1, waiting for transfers between devices: 187 us -> 149 us  [on_device(): lax.psum((grad_flip * scale, plan_step_gradient * scale, grad_gain_tanner...]
    psum x0 -> x1, waiting for transfers between devices: none -> 28.2 us  [on_device(): lax.psum(lax.psum((grad_flip * scale, plan_step_gradient * scale, grad_ga...]
    psum x1, blocking collectives: 75 us -> 62.4 us  [on_device(): lax.psum((grad_flip * scale, plan_step_gradient * scale, grad_gain_tanner...]
    unnamed x89 -> x87, local copies, waits for them, and re-layouts: 19.3 us -> 19.5 us
  transfers between devices with their start and end apart: 5 -> 6, of which waited for: 3 -> 4; matrix products, arithmetic and copies ran while one was open for 1% -> 1% of each run, Pallas kernels for 0% -> 0%
where the time goes in v1:
time: 409 us; the launch traced here: 403 us
  waiting for transfers between devices  186 us (45%)
  blocking collectives  119 us (29%)
  matrix products  32.1 us (8%)
  between operations  26.5 us (6%)
  local copies, waits for them, and re-layouts  23.3 us (6%)
  starting transfers between devices  9.22 us (2%)
  other arithmetic  6.51 us (2%)
    psum x1, waiting for transfers between devices, on_device(): lax.psum((grad_flip * scale, plan_step_gradient * scale, grad_gain_tanner...  149 us
    psum x1, blocking collectives, on_device(): lax.psum((grad_flip * scale, plan_step_gradient * scale, grad_gain_tanner...  62.4 us
    psum x1, blocking collectives, on_device(): lax.psum(lax.psum((grad_flip * scale, plan_step_gradient * scale, grad_ga...  56.6 us
    psum x1, waiting for transfers between devices, on_device(): lax.psum(lax.psum((grad_flip * scale, plan_step_gradient * scale, grad_ga...  28.2 us
    unnamed x87, local copies, waits for them, and re-layouts  19.5 us
    dot_general x34, matrix products, head_total(): lax.dot_general(product, block, (((product.ndim - 1,), (0,)), ((), ())),...  15.3 us
    ppermute x4, starting transfers between devices, shifted(): return lax.ppermute(x, axis, [(i, (i + by) % count) for i in range(count)])  9.14 us
    ppermute x4, waiting for transfers between devices, shifted(): return lax.ppermute(x, axis, [(i, (i + by) % count) for i in range(count)])  8.64 us
  transfers between devices with their start and end apart: 6, of which 4 were waited for; matrix products, arithmetic and copies ran while one was open for 1% of the time, Pallas kernels for 0%

profile of v1, /device:TPU:2, one launch (start us, length us, event | category | flops | bytes accessed | tf_op | source)
XLA Modules:
  0.0 402.7 jit_solution(13223422837887103489)
XLA Ops:
  8.7 1.3 multiply_reduce_fusion.9
  11.4 6.9 %collective-permute-start = (bf16[4,8,8,512]{3,2,1,0:T(8,128)(2,1)S(1)}, bf16[4,8,8,512]{3,2,1,0:T(8,128)(2,1)S(1)}, u32[]{:S(2)}, u32[]{:S(2)}) collective-permute-start(bf16[4,8,8,512]{3,2,1,0:T(8,128)(2,1)S(1)} %get-tuple-element.175), channel_id=1, source_target_pairs={{0,240},{16,0},{32,16},{48,32},{64,48},{80,64},{96,80},{112,96},{1... | collective-permute-start | bytes 786440 | tf_op jit(solution)/shard_map/ppermute | solution.py:20
  18.4 2.0 collective-permute-start.1
  47.6 1.0 fusion.12
  53.2 1.3 fusion.2
  54.4 1.1 multiply_reduce_fusion.1
  55.7 1.9 fusion.472
  60.6 1.4 fusion.1
  62.0 1.5 fusion
  63.5 1.6 fusion.485
  65.3 0.9 dynamic_update_slice.22
  66.2 1.2 add_add_fusion.1
  67.4 1.0 add_any.332
  68.4 1.2 add_add_fusion
  76.5 2.4 collective-permute-done.3
  78.9 6.3 %collective-permute-done.2 = bf16[4,8,8,512]{3,2,1,0:T(8,128)(2,1)S(1)} collective-permute-done((bf16[4,8,8,512]{3,2,1,0:T(8,128)(2,1)S(1)}, bf16[4,8,8,512]{3,2,1,0:T(8,128)(2,1)S(1)}, u32[]{:S(2)}, u32[]{:S(2)}) %collective-permute-start.2) | collective-permute-done | bytes 262176 | tf_op jit(solution)/shard_map/ppermute | solution.py:20
  85.3 1.1 fusion.4
  86.5 149.2 %all-reduce.56.cloned.1.call-done = (f32[256,256]{1,0:T(8,128)}, f32[256,512]{1,0:T(8,128)}, f32[256,256]{1,0:T(8,128)}, f32[256,768]{1,0:T(8,128)}, f32[256,256...) async-done(((f32[256,256]{1,0:T(8,128)}, f32[256,512]{1,0:T(8,128)}, f32[256,256]{1,0:T(8,128)}, f32[256,768]{1,0:T(8,128)}, f32[256,256]{1,0:T(8,128)}, ...) | async-done | bytes 4194320 | tf_op jit(solution)/shard_map/psum | solution.py:204
  240.7 62.4 %all-reduce.49 = (f32[256]{0:T(256)S(1)}, f32[8,256]{1,0:T(8,128)S(1)}, f32[256]{0:T(256)S(1)}, f32[256]{0:T(256)S(1)}, f32[256]{0:T(256)S(1)}) all-reduce(f32[256]{0:T(256)S(1)} %broadcast_multiply_fusion.3, f32[8,256]{1,0:T(8,128)S(1)} %fusion.26, f32[256]{0:T(256)S(1)} %broadcast_multiply_fusion.2, ...), channel_id=1, replica_groups=mesh['gx'=16,'gy'=16] {'gx'}, use_global_device_ids=true, to_apply=%region_7.8 | all-reduce | flops 3072 | bytes 24576 | tf_op jit(solution)/shard_map/psum | solution.py:204
  303.1 56.6 %all-reduce.47 = (f32[256]{0:T(256)}, f32[8,256]{1,0:T(8,128)}, f32[256]{0:T(256)}, f32[256]{0:T(256)}, f32[256]{0:T(256)}) all-reduce(f32[256]{0:T(256)S(1)} %get-tuple-element.71, f32[8,256]{1,0:T(8,128)S(1)} %get-tuple-element.72, f32[256]{0:T(256)S(1)} %get-tuple-element.73, ...), channel_id=1, replica_groups=mesh['gx'=16,'gy'=16] {'gy'}, use_global_device_ids=true, to_apply=%region_8.9 | all-reduce | flops 3072 | bytes 24576 | tf_op jit(solution)/shard_map/psum | solution.py:203
  359.8 28.2 %all-reduce.54.cloned.1.call-done = (f32[256,256]{1,0:T(8,128)}, f32[256,512]{1,0:T(8,128)}, f32[256,256]{1,0:T(8,128)}, f32[256,768]{1,0:T(8,128)}, f32[256,256...) async-done(((f32[256,256]{1,0:T(8,128)}, f32[256,512]{1,0:T(8,128)}, f32[256,256]{1,0:T(8,128)}, f32[256,768]{1,0:T(8,128)}, f32[256,256]{1,0:T(8,128)}, ...) | async-done | bytes 4194320 | tf_op jit(solution)/shard_map/psum | solution.py:203
  388.0 1.7 copy.69
  393.3 1.0 copy.74
  394.9 1.0 copy.75
  (178 shorter events, 42.2 us)
Async XLA Ops:
  7.2 36.7 %copy-start = (bf16[256,1024]{1,0:T(8,128)(2,1)S(1)}, bf16[256,1024]{1,0:T(8,128)(2,1)}, u32[]{:S(2)}) copy-start(bf16[256,1024]{1,0:T(8,128)(2,1)} %param.39) | copy-start | bytes 1572868
  7.2 1.4 copy-start.29
  7.2 1.4 copy-start.37
  7.2 1.4 copy-start.34
  7.2 228.5 %all-reduce.56.cloned.1.call-start = ((), (), s32[]{:S(2)}) async-start(), calls=%async_computation.1 | async-start | bytes 8388608 | tf_op jit(solution)/shard_map/psum | solution.py:204
  8.6 1.9 copy-start.33
  10.0 1.2 copy-start.4
  11.2 21.5 %copy-start.10 = (bf16[256,256]{1,0:T(8,128)(2,1)S(1)}, bf16[256,256]{1,0:T(8,128)(2,1)}, u32[]{:S(2)}) copy-start(bf16[256,256]{1,0:T(8,128)(2,1)} %param.32) | copy-start | bytes 393220
  11.4 9.0 %copy-start.32 = (s32[6,2]{0,1:T(2,128)S(1)}, s32[6,2]{0,1:T(2,128)}, u32[]{:S(2)}) copy-start(s32[6,2]{0,1:T(2,128)} %param.28) | copy-start | bytes 148
  11.4 21.4 %collective-permute-start = (bf16[4,8,8,512]{3,2,1,0:T(8,128)(2,1)S(1)}, bf16[4,8,8,512]{3,2,1,0:T(8,128)(2,1)S(1)}, u32[]{:S(2)}, u32[]{:S(2)}) collective-permute-start(bf16[4,8,8,512]{3,2,1,0:T(8,128)(2,1)S(1)} %get-tuple-element.175), channel_id=1, source_target_pairs={{0,240},{16,0},{32,16},{48,32},{64,48},{80,64},{96,80},{112,96},{1... | collective-permute-start | bytes 786440 | tf_op jit(solution)/shard_map/ppermute | solution.py:20
  18.4 14.6 %collective-permute-start.1 = (bf16[4,8,8,512]{3,2,1,0:T(8,128)(2,1)S(1)}, bf16[4,8,8,512]{3,2,1,0:T(8,128)(2,1)S(1)}, u32[]{:S(2)}, u32[]{:S(2)}) collective-permute-start(bf16[4,8,8,512]{3,2,1,0:T(8,128)(2,1)S(1)} %get-tuple-element.175), channel_id=1, source_target_pairs={{0,15},{1,0},{2,1},{3,2},{4,3},{5,4},{6,5},{7,6},{8,7},{9,8},{10,9... | collective-permute-start | bytes 786440 | tf_op jit(solution)/shard_map/ppermute | solution.py:20
  44.5 1.1 copy-start.39
  70.6 8.3 %collective-permute-start.3 = (bf16[4,8,8,512]{3,2,1,0:T(8,128)(2,1)S(1)}, bf16[4,8,8,512]{3,2,1,0:T(8,128)(2,1)S(1)}, u32[]{:S(2)}, u32[]{:S(2)}) collective-permute-start(bf16[4,8,8,512]{3,2,1,0:T(8,128)(2,1)S(1)} %split.34), channel_id=1, source_target_pairs={{0,1},{1,2},{2,3},{3,4},{4,5},{5,6},{6,7},{7,8},{8,9},{9,10},{10,1... | collective-permute-start | bytes 786440 | tf_op jit(solution)/shard_map/ppermute | solution.py:20
  70.7 1.0 copy-start.20
  73.8 11.4 %collective-permute-start.2 = (bf16[4,8,8,512]{3,2,1,0:T(8,128)(2,1)S(1)}, bf16[4,8,8,512]{3,2,1,0:T(8,128)(2,1)S(1)}, u32[]{:S(2)}, u32[]{:S(2)}) collective-permute-start(bf16[4,8,8,512]{3,2,1,0:T(8,128)(2,1)S(1)} %split.35), channel_id=1, source_target_pairs={{0,16},{16,32},{32,48},{48,64},{64,80},{80,96},{96,112},{112,128},... | collective-permute-start | bytes 786440 | tf_op jit(solution)/shard_map/ppermute | solution.py:20
  75.6 9.6 %copy-start.15 = (f32[4,8,8,256]{3,2,1,0:T(8,128)S(1)}, f32[4,8,8,256]{3,2,1,0:T(8,128)}, u32[]{:S(2)}) copy-start(f32[4,8,8,256]{3,2,1,0:T(8,128)} %get-tuple-element.117) | copy-start | bytes 786436
  86.4 301.5 %all-reduce.54.cloned.1.call-start = ((), (), s32[]{:S(2)}) async-start(), calls=%async_computation | async-start | bytes 8388608 | tf_op jit(solution)/shard_map/psum | solution.py:203
  235.7 1.4 copy-start.11
  388.0 1.7 copy-start.8
  389.7 1.1 copy-start.17
  389.7 1.8 copy-start.6
  391.5 1.1 copy-start.16
  391.5 1.8 copy-start.2
  393.3 1.6 copy-start.1
  (22 other events, 17.7 us)
Sparse Core Ops, SparseCore 0:
  86.5 149.1 all-reduce.55
  238.9 148.9 all-reduce.53
